TPU v7x, 128 devices: a whole 4x4x4 slice. The times are simulated.
128 devices in a mesh: lat: 8 (over x_lo, z), lon: 16 (over x_hi, y, core).
Axes of the slice: x: 4 (x_hi: 2, x_lo: 2; x = x_hi * 2 + x_lo), y: 4, z: 4, core: 2. Of those that a mesh axis runs over, the one named last changes fastest.
Arguments:
- features: bfloat16 [32, 1024, 2048], P(None, 'lat', 'lon'), may hold values from -6 to 6
- cotangent: bfloat16 [32, 1024, 2048], P(None, 'lat', 'lon'), may hold values from -6 to 6
- sea_mask: int32 [1024, 2048], P('lat', 'lon'), may hold values 0 or 1
- weights: bfloat16 [5, 32, 32], replicated, may hold values from -1 to 1
Outputs:
- feature_grad: bfloat16 [32, 1024, 2048], P(None, 'lat', 'lon')
- weight_grad: float32 [5, 32, 32], replicated
Inputs may be any that keep to these rules, and one draw needn't show every extreme that they name: `sea_mask`: 1 marks a sea cell, 0 a land cell.
All inputs are finite; a program needn't handle non-finite values. No bound on the sum of `sea_mask` on one device may be relied on, other than what follows from the above.
Results may differ from a plain program's by a relative error of at most 0.0069.
Values sent between devices are 32-bit elements; how exact they have to be, the bound alone decides.
A program may use at most 128 MiB of HBM per device.

v0:
```python
import math
import jax
import jax.numpy as jnp
from jax import lax
from jax.sharding import PartitionSpec as P

K = 4
NEIGHBOURS = ((0, -1), (0, 1), (-1, 0), (1, 0), (-1, 1), (1, -1))


def padded_2(cells, sides, width, closed):
    for axis, dim in sides:
        count = lax.axis_size(axis)
        ends = count if closed else count - 1
        head = lax.slice_in_dim(cells, 0, width, axis=dim)
        tail = lax.slice_in_dim(cells, cells.shape[dim] - width, cells.shape[dim], axis=dim)
        cells = jnp.concatenate(
            [
                lax.ppermute(tail, axis, [(i, (i + 1) % count) for i in range(ends)]),
                cells,
                lax.ppermute(head, axis, [((i + 1) % count, i) for i in range(ends)]),
            ],
            axis=dim,
        )
    return cells


def neigh_sum(padded, outer_pad, inner_pad):
    row_count = padded.shape[-2] - 2 * (outer_pad - inner_pad)
    col_count = padded.shape[-1] - 2 * (outer_pad - inner_pad)
    base = outer_pad - inner_pad
    summed = None
    for step_row, step_col in NEIGHBOURS:
        shifted = padded[
            ...,
            base + step_row : base + step_row + row_count,
            base + step_col : base + step_col + col_count,
        ]
        summed = shifted if summed is None else summed + shifted
    return summed


def extend(cells_in, depth_cells):
    widened = padded_2(cells_in, (("lon", 2),), depth_cells, True)
    return padded_2(widened, (("lat", 1),), depth_cells, False)


def extend_flags(flag_cells, depth_cells):
    widened = padded_2(flag_cells, (("lon", 1),), depth_cells, True)
    return padded_2(widened, (("lat", 0),), depth_cells, False)


def local(features, cotangent, sea_mask, weights):
    flags_three = extend_flags(sea_mask, 3).astype(jnp.float32)
    degree = neigh_sum(flags_three, 3, 2)
    scale_two = flags_three[1:-1, 1:-1] / jnp.sqrt(jnp.maximum(degree, 1.0))
    scale_one = scale_two[1:-1, 1:-1]
    scale_zero = scale_two[2:-2, 2:-2]
    sea_cells = sea_mask.astype(jnp.float32)

    def laplace(cells_in):
        padded = extend(cells_in, 1)
        return -scale_zero * neigh_sum(scale_one * padded, 1, 0)

    initial = sea_cells * features.astype(jnp.float32)

    def keep_visit(carried, term):
        return carried + (term.astype(jnp.bfloat16),)

    carried = ()
    carried = keep_visit(carried, initial)
    previous = initial
    current = laplace(initial)
    carried = keep_visit(carried, current)
    for order_k in range(2, K + 1):
        advanced = 2.0 * laplace(current) - previous
        carried = keep_visit(carried, advanced)
        previous, current = (current, advanced)
    mixed = jnp.zeros(features.shape, jnp.float32)
    for index_k in range(K + 1):
        mixed = mixed + jnp.einsum(
            "cd,cij->dij", weights[index_k], carried[index_k], preferred_element_type=jnp.float32
        )
    activated = jnp.tanh(mixed)
    grad_mix = (cotangent.astype(jnp.float32) * (1.0 - activated * activated)).astype(jnp.bfloat16)
    weight_terms = jnp.stack(
        [
            jnp.einsum("cij,dij->cd", kept, grad_mix, preferred_element_type=jnp.float32)
            for kept in carried
        ]
    )
    summed = lax.psum(weight_terms, ("lat", "lon"))
    grid_cells = features.shape[1] * lax.axis_size("lat") * features.shape[2] * lax.axis_size("lon")
    weight_grad = summed * (1.0 / math.sqrt(grid_cells))

    def project(index_k):
        return jnp.einsum(
            "cd,dij->cij", weights[index_k], grad_mix, preferred_element_type=jnp.float32
        )

    upper_one = project(K)
    upper_two = jnp.zeros(features.shape, jnp.float32)
    for index_k in range(K - 1, 0, -1):
        fresh = project(index_k) + 2.0 * laplace(upper_one) - upper_two
        upper_two, upper_one = (upper_one, fresh)
    result = project(0) + laplace(upper_one) - upper_two
    feature_grad = (sea_cells * result).astype(jnp.bfloat16)
    return (feature_grad, weight_grad)


def solution(mesh):
    placed = (P(None, "lat", "lon"), P(None, "lat", "lon"), P("lat", "lon"), P())
    return jax.shard_map(
        local, mesh=mesh, in_specs=placed, out_specs=(P(None, "lat", "lon"), P()), check_vma=False
    )
```

profile of v0, /device:TPU:96, one launch (start us, length us, event | category | flops | bytes accessed | tf_op | source)
XLA Modules:
  0.0 407.8 jit_solution(406099193958542431)
XLA Ops:
  1.7 5.3 %collective-permute-start.1 = (s32[128,3]{1,0:T(8,128)S(1)}, s32[128,3]{1,0:T(8,128)S(1)}, u32[]{:S(2)}, u32[]{:S(2)}) collective-permute-start(s32[128,3]{1,0:T(8,128)S(1)} %get-tuple-element.41), channel_id=1, source_target_pairs={{1,0},{2,1},{3,2},{4,3},{5,4},{6,5},{7,6},{8,7},{9,8},{10,9},{11,1... | collective-permute-start | bytes 4616 | tf_op jit(solution)/shard_map/ppermute | solution.py:21
  12.0 3.8 collective-permute-start.3
  24.0 5.4 %collective-permute-start.5 = (f32[32,128,1]{1,0,2:T(8,128)S(1)}, f32[32,128,1]{1,0,2:T(8,128)S(1)}, u32[]{:S(2)}, u32[]{:S(2)}) collective-permute-start(f32[32,128,1]{1,0,2:T(8,128)S(1)} %copy.23), channel_id=1, source_target_pairs={{1,0},{2,1},{3,2},{4,3},{5,4},{6,5},{7,6},{8,7},{9,8},{10,9},{11,1... | collective-permute-start | bytes 49160 | tf_op jit(solution)/shard_map/ppermute | solution.py:21
  36.5 4.3 %collective-permute-start.6 = (f32[32,1,130]{2,0,1:T(8,128)S(1)}, f32[32,1,130]{2,0,1:T(8,128)S(1)}, u32[]{:S(2)}, u32[]{:S(2)}) collective-permute-start(f32[32,1,130]{2,0,1:T(8,128)S(1)} %get-tuple-element.20), channel_id=1, source_target_pairs={{0,16},{16,32},{32,48},{48,64},{64,80},{80,96},{96,112},{1,17},{17... | collective-permute-start | bytes 49928 | tf_op jit(solution)/shard_map/ppermute | solution.py:19
  43.1 5.6 %collective-permute-done.7 = f32[32,1,130]{2,0,1:T(8,128)S(1)} collective-permute-done((f32[32,1,130]{2,0,1:T(8,128)S(1)}, f32[32,1,130]{2,0,1:T(8,128)S(1)}, u32[]{:S(2)}, u32[]{:S(2)}) %collective-permute-start.7) | collective-permute-done | bytes 16672 | tf_op jit(solution)/shard_map/ppermute | solution.py:21
  61.6 5.4 %collective-permute-start.9 = (f32[32,128,1]{1,0,2:T(8,128)S(1)}, f32[32,128,1]{1,0,2:T(8,128)S(1)}, u32[]{:S(2)}, u32[]{:S(2)}) collective-permute-start(f32[32,128,1]{1,0,2:T(8,128)S(1)} %copy.28), channel_id=1, source_target_pairs={{1,0},{2,1},{3,2},{4,3},{5,4},{6,5},{7,6},{8,7},{9,8},{10,9},{11,1... | collective-permute-start | bytes 49160 | tf_op jit(solution)/shard_map/ppermute | solution.py:21
  75.9 4.3 %collective-permute-start.11 = (f32[32,1,130]{2,0,1:T(8,128)S(1)}, f32[32,1,130]{2,0,1:T(8,128)S(1)}, u32[]{:S(2)}, u32[]{:S(2)}) collective-permute-start(f32[32,1,130]{2,0,1:T(8,128)S(1)} %get-tuple-element.19), channel_id=1, source_target_pairs={{16,0},{32,16},{48,32},{64,48},{80,64},{96,80},{112,96},{17,1},{33... | collective-permute-start | bytes 49928 | tf_op jit(solution)/shard_map/ppermute | solution.py:21
  80.1 3.8 collective-permute-done.11
  86.4 4.1 %fusion.25 = f32[32,128,128]{2,0,1:T(8,128)S(1)} fusion(f32[32,130,130]{2,0,1:T(8,128)S(1)} %maximum_multiply_fusion.1, f32[128,128]{1,0:T(8,128)S(1)} %slice_negate_fusion, bf16[32,128,128]{2,1,0:T(8,128)(2,1)S(1)} %copy-done.33, f32[128,128]{1,0:T(8,128)S(1)} %convert_element_type.33), kind=kLoop, calls=%fused_computation.64 | loop fusion | flops 5242880 | bytes 15859712 | tf_op jit(solution)/shard_map/sub | solution.py:76
  98.7 5.4 %collective-permute-start.13 = (f32[32,128,1]{1,0,2:T(8,128)S(1)}, f32[32,128,1]{1,0,2:T(8,128)S(1)}, u32[]{:S(2)}, u32[]{:S(2)}) collective-permute-start(f32[32,128,1]{1,0,2:T(8,128)S(1)} %copy.33), channel_id=1, source_target_pairs={{1,0},{2,1},{3,2},{4,3},{5,4},{6,5},{7,6},{8,7},{9,8},{10,9},{11,1... | collective-permute-start | bytes 49160 | tf_op jit(solution)/shard_map/ppermute | solution.py:21
  115.0 4.6 %collective-permute-start.15 = (f32[32,1,130]{2,0,1:T(8,128)S(1)}, f32[32,1,130]{2,0,1:T(8,128)S(1)}, u32[]{:S(2)}, u32[]{:S(2)}) collective-permute-start(f32[32,1,130]{2,0,1:T(8,128)S(1)} %get-tuple-element.17), channel_id=1, source_target_pairs={{16,0},{32,16},{48,32},{64,48},{80,64},{96,80},{112,96},{17,1},{33... | collective-permute-start | bytes 49928 | tf_op jit(solution)/shard_map/ppermute | solution.py:21
  123.1 3.9 maximum_multiply_fusion.2
  127.0 11.8 %fusion.22 = f32[32,128,128]{2,0,1:T(8,128)S(1)} fusion(f32[32,130,130]{2,0,1:T(8,128)} %maximum_multiply_fusion.2, f32[128,128]{1,0:T(8,128)S(1)} %slice_negate_fusion, f32[32,130,130]{2,0,1:T(8,128)S(1)} %bitcast.102), kind=kLoop, calls=%fused_computation.56 | loop fusion | flops 7340032 | bytes 27328512 | tf_op jit(solution)/shard_map/sub | solution.py:76
  147.0 5.4 %collective-permute-start.17 = (f32[32,128,1]{1,0,2:T(8,128)S(1)}, f32[32,128,1]{1,0,2:T(8,128)S(1)}, u32[]{:S(2)}, u32[]{:S(2)}) collective-permute-start(f32[32,128,1]{1,0,2:T(8,128)S(1)} %copy.38), channel_id=1, source_target_pairs={{1,0},{2,1},{3,2},{4,3},{5,4},{6,5},{7,6},{8,7},{9,8},{10,9},{11,1... | collective-permute-start | bytes 49160 | tf_op jit(solution)/shard_map/ppermute | solution.py:21
  163.4 3.9 collective-permute-start.19
  171.5 3.8 maximum_multiply_fusion.3
  175.4 10.2 %fusion.19 = bf16[32,128,128]{2,0,1:T(8,128)(2,1)S(1)} fusion(f32[32,128,128]{2,0,1:T(8,128)S(1)} %fusion.25, f32[32,130,130]{2,0,1:T(8,128)} %maximum_multiply_fusion.3, f32[128,128]{1,0:T(8,128)S(1)} %slice_negate_fusion), kind=kLoop, calls=%fused_computation.48 | loop fusion | flops 4718592 | bytes 15794176 | tf_op jit(solution)/shard_map/convert_element_type | solution.py:68
  185.6 5.6 %fusion.27 = bf16[32,128,128]{2,0,1:T(8,128)(2,1)S(1)} fusion(f32[128,128,32]{1,2,0:T(8,128)} %fusion.34, f32[128,128,32]{1,2,0:T(8,128)} %fusion.37, f32[128,128,32]{1,2,0:T(8,128)} %fusion.43, f32[128,128,32]{1,2,0:T(8,128)} %fusion.40, bf16[32,128,128]{2,0,1:T(8,128)(2,1)S(1)} %fusion.19, bf16[32,128,128]{2,1,0:T(8,128)(2,1)} %param.5, ...), kind=kOutput, calls=%fused_computation.76 | convolution fusion | flops 38273024 | bytes 11542528 | tf_op jit(solution)/shard_map/cd,cij->dij/dot_general | solution.py:81
  199.8 5.4 %collective-permute-start.21 = (f32[32,128,1]{1,0,2:T(8,128)S(1)}, f32[32,128,1]{1,0,2:T(8,128)S(1)}, u32[]{:S(2)}, u32[]{:S(2)}) collective-permute-start(f32[32,128,1]{1,0,2:T(8,128)S(1)} %copy.48), channel_id=1, source_target_pairs={{1,0},{2,1},{3,2},{4,3},{5,4},{6,5},{7,6},{8,7},{9,8},{10,9},{11,1... | collective-permute-start | bytes 49160 | tf_op jit(solution)/shard_map/ppermute | solution.py:21
  214.5 4.0 collective-permute-start.23
  218.4 3.9 collective-permute-done.23
  235.3 5.4 %collective-permute-start.25 = (f32[32,128,1]{1,0,2:T(8,128)S(1)}, f32[32,128,1]{1,0,2:T(8,128)S(1)}, u32[]{:S(2)}, u32[]{:S(2)}) collective-permute-start(f32[32,128,1]{1,0,2:T(8,128)S(1)} %copy.52), channel_id=1, source_target_pairs={{1,0},{2,1},{3,2},{4,3},{5,4},{6,5},{7,6},{8,7},{9,8},{10,9},{11,1... | collective-permute-start | bytes 49160 | tf_op jit(solution)/shard_map/ppermute | solution.py:21
  252.5 4.3 %collective-permute-start.27 = (f32[32,1,130]{2,0,1:T(8,128)S(1)}, f32[32,1,130]{2,0,1:T(8,128)S(1)}, u32[]{:S(2)}, u32[]{:S(2)}) collective-permute-start(f32[32,1,130]{2,0,1:T(8,128)S(1)} %get-tuple-element.11), channel_id=1, source_target_pairs={{16,0},{32,16},{48,32},{64,48},{80,64},{96,80},{112,96},{17,1},{33... | collective-permute-start | bytes 49928 | tf_op jit(solution)/shard_map/ppermute | solution.py:21
  273.3 5.4 %collective-permute-start.29 = (f32[32,128,1]{1,0,2:T(8,128)S(1)}, f32[32,128,1]{1,0,2:T(8,128)S(1)}, u32[]{:S(2)}, u32[]{:S(2)}) collective-permute-start(f32[32,128,1]{1,0,2:T(8,128)S(1)} %copy.56), channel_id=1, source_target_pairs={{1,0},{2,1},{3,2},{4,3},{5,4},{6,5},{7,6},{8,7},{9,8},{10,9},{11,1... | collective-permute-start | bytes 49160 | tf_op jit(solution)/shard_map/ppermute | solution.py:21
  288.7 4.1 %collective-permute-start.31 = (f32[32,1,130]{2,0,1:T(8,128)S(1)}, f32[32,1,130]{2,0,1:T(8,128)S(1)}, u32[]{:S(2)}, u32[]{:S(2)}) collective-permute-start(f32[32,1,130]{2,0,1:T(8,128)S(1)} %get-tuple-element.9), channel_id=1, source_target_pairs={{16,0},{32,16},{48,32},{64,48},{80,64},{96,80},{112,96},{17,1},{33... | collective-permute-start | bytes 49928 | tf_op jit(solution)/shard_map/ppermute | solution.py:21
  306.9 3.2 copy.60
  310.1 5.3 %collective-permute-start.33 = (f32[32,128,1]{1,0,2:T(8,128)}, f32[32,128,1]{1,0,2:T(8,128)}, u32[]{:S(2)}, u32[]{:S(2)}) collective-permute-start(f32[32,128,1]{1,0,2:T(8,128)} %copy.60), channel_id=1, source_target_pairs={{1,0},{2,1},{3,2},{4,3},{5,4},{6,5},{7,6},{8,7},{9,8},{10,9},{11,1... | collective-permute-start | bytes 49160 | tf_op jit(solution)/shard_map/ppermute | solution.py:21
  317.7 62.9 %psum.7 = f32[5,32,32]{2,1,0:T(8,128)S(1)} all-reduce(f32[5,32,32]{2,1,0:T(8,128)} %fusion.28), channel_id=1, replica_groups=mesh['lat'=8,'lon'=16] {'lat','lon'}, use_global_device_ids=true, to_apply=%region_0.0 | all-reduce | flops 5120 | bytes 40960 | tf_op jit(solution)/shard_map/psum | solution.py:92
  380.7 3.6 copy.61
  384.3 3.6 copy.62
  388.9 4.4 %collective-permute-start.34 = (f32[32,1,130]{2,0,1:T(8,128)S(1)}, f32[32,1,130]{2,0,1:T(8,128)S(1)}, u32[]{:S(2)}, u32[]{:S(2)}) collective-permute-start(f32[32,1,130]{2,0,1:T(8,128)S(1)} %get-tuple-element.6), channel_id=1, source_target_pairs={{0,16},{16,32},{32,48},{48,64},{64,80},{80,96},{96,112},{1,17},{17... | collective-permute-start | bytes 49928 | tf_op jit(solution)/shard_map/ppermute | solution.py:19
  396.1 5.1 %collective-permute-done.35 = f32[32,1,130]{2,0,1:T(8,128)S(1)} collective-permute-done((f32[32,1,130]{2,0,1:T(8,128)S(1)}, f32[32,1,130]{2,0,1:T(8,128)S(1)}, u32[]{:S(2)}, u32[]{:S(2)}) %collective-permute-start.35) | collective-permute-done | bytes 16672 | tf_op jit(solution)/shard_map/ppermute | solution.py:21
  (205 shorter events, 189.0 us)
Async XLA Ops:
  1.7 8.2 %collective-permute-start = (s32[128,3]{1,0:T(8,128)S(1)}, s32[128,3]{1,0:T(8,128)S(1)}, u32[]{:S(2)}, u32[]{:S(2)}) collective-permute-start(s32[128,3]{1,0:T(8,128)S(1)} %get-tuple-element.40), channel_id=1, source_target_pairs={{0,1},{1,2},{2,3},{3,4},{4,5},{5,6},{6,7},{7,8},{8,9},{9,10},{10,1... | collective-permute-start | bytes 4616 | tf_op jit(solution)/shard_map/ppermute | solution.py:19
  1.7 8.2 %collective-permute-start.1 = (s32[128,3]{1,0:T(8,128)S(1)}, s32[128,3]{1,0:T(8,128)S(1)}, u32[]{:S(2)}, u32[]{:S(2)}) collective-permute-start(s32[128,3]{1,0:T(8,128)S(1)} %get-tuple-element.41), channel_id=1, source_target_pairs={{1,0},{2,1},{3,2},{4,3},{5,4},{6,5},{7,6},{8,7},{9,8},{10,9},{11,1... | collective-permute-start | bytes 4616 | tf_op jit(solution)/shard_map/ppermute | solution.py:21
  10.0 19.4 %collective-permute-start.2 = (s32[3,134]{1,0:T(4,128)S(1)}, s32[3,134]{1,0:T(4,128)S(1)}, u32[]{:S(2)}, u32[]{:S(2)}) collective-permute-start(s32[3,134]{1,0:T(4,128)S(1)} %get-tuple-element.38), channel_id=1, source_target_pairs={{0,16},{16,32},{32,48},{48,64},{64,80},{80,96},{96,112},{1,17},{17... | collective-permute-start | bytes 4832 | tf_op jit(solution)/shard_map/ppermute | solution.py:19
  12.0 17.3 %collective-permute-start.3 = (s32[3,134]{1,0:T(4,128)S(1)}, s32[3,134]{1,0:T(4,128)S(1)}, u32[]{:S(2)}, u32[]{:S(2)}) collective-permute-start(s32[3,134]{1,0:T(4,128)S(1)} %get-tuple-element.39), channel_id=1, source_target_pairs={{16,0},{32,16},{48,32},{64,48},{80,64},{96,80},{112,96},{17,1},{33... | collective-permute-start | bytes 4832 | tf_op jit(solution)/shard_map/ppermute | solution.py:21
  21.3 8.5 %collective-permute-start.4 = (f32[32,128,1]{1,0,2:T(8,128)S(1)}, f32[32,128,1]{1,0,2:T(8,128)S(1)}, u32[]{:S(2)}, u32[]{:S(2)}) collective-permute-start(f32[32,128,1]{1,0,2:T(8,128)S(1)} %copy.22), channel_id=1, source_target_pairs={{0,1},{1,2},{2,3},{3,4},{4,5},{5,6},{6,7},{7,8},{8,9},{9,10},{10,1... | collective-permute-start | bytes 49160 | tf_op jit(solution)/shard_map/ppermute | solution.py:19
  24.0 8.7 %collective-permute-start.5 = (f32[32,128,1]{1,0,2:T(8,128)S(1)}, f32[32,128,1]{1,0,2:T(8,128)S(1)}, u32[]{:S(2)}, u32[]{:S(2)}) collective-permute-start(f32[32,128,1]{1,0,2:T(8,128)S(1)} %copy.23), channel_id=1, source_target_pairs={{1,0},{2,1},{3,2},{4,3},{5,4},{6,5},{7,6},{8,7},{9,8},{10,9},{11,1... | collective-permute-start | bytes 49160 | tf_op jit(solution)/shard_map/ppermute | solution.py:21
  40.8 7.9 %collective-permute-start.7 = (f32[32,1,130]{2,0,1:T(8,128)S(1)}, f32[32,1,130]{2,0,1:T(8,128)S(1)}, u32[]{:S(2)}, u32[]{:S(2)}) collective-permute-start(f32[32,1,130]{2,0,1:T(8,128)S(1)} %get-tuple-element.21), channel_id=1, source_target_pairs={{16,0},{32,16},{48,32},{64,48},{80,64},{96,80},{112,96},{17,1},{33... | collective-permute-start | bytes 49928 | tf_op jit(solution)/shard_map/ppermute | solution.py:21
  58.9 8.1 %collective-permute-start.8 = (f32[32,128,1]{1,0,2:T(8,128)S(1)}, f32[32,128,1]{1,0,2:T(8,128)S(1)}, u32[]{:S(2)}, u32[]{:S(2)}) collective-permute-start(f32[32,128,1]{1,0,2:T(8,128)S(1)} %copy.27), channel_id=1, source_target_pairs={{0,1},{1,2},{2,3},{3,4},{4,5},{5,6},{6,7},{7,8},{8,9},{9,10},{10,1... | collective-permute-start | bytes 49160 | tf_op jit(solution)/shard_map/ppermute | solution.py:19
  61.6 8.3 %collective-permute-start.9 = (f32[32,128,1]{1,0,2:T(8,128)S(1)}, f32[32,128,1]{1,0,2:T(8,128)S(1)}, u32[]{:S(2)}, u32[]{:S(2)}) collective-permute-start(f32[32,128,1]{1,0,2:T(8,128)S(1)} %copy.28), channel_id=1, source_target_pairs={{1,0},{2,1},{3,2},{4,3},{5,4},{6,5},{7,6},{8,7},{9,8},{10,9},{11,1... | collective-permute-start | bytes 49160 | tf_op jit(solution)/shard_map/ppermute | solution.py:21
  75.9 8.0 %collective-permute-start.11 = (f32[32,1,130]{2,0,1:T(8,128)S(1)}, f32[32,1,130]{2,0,1:T(8,128)S(1)}, u32[]{:S(2)}, u32[]{:S(2)}) collective-permute-start(f32[32,1,130]{2,0,1:T(8,128)S(1)} %get-tuple-element.19), channel_id=1, source_target_pairs={{16,0},{32,16},{48,32},{64,48},{80,64},{96,80},{112,96},{17,1},{33... | collective-permute-start | bytes 49928 | tf_op jit(solution)/shard_map/ppermute | solution.py:21
  96.0 10.3 %collective-permute-start.12 = (f32[32,128,1]{1,0,2:T(8,128)S(1)}, f32[32,128,1]{1,0,2:T(8,128)S(1)}, u32[]{:S(2)}, u32[]{:S(2)}) collective-permute-start(f32[32,128,1]{1,0,2:T(8,128)S(1)} %copy.32), channel_id=1, source_target_pairs={{0,1},{1,2},{2,3},{3,4},{4,5},{5,6},{6,7},{7,8},{8,9},{9,10},{10,1... | collective-permute-start | bytes 49160 | tf_op jit(solution)/shard_map/ppermute | solution.py:19
  98.7 10.5 %collective-permute-start.13 = (f32[32,128,1]{1,0,2:T(8,128)S(1)}, f32[32,128,1]{1,0,2:T(8,128)S(1)}, u32[]{:S(2)}, u32[]{:S(2)}) collective-permute-start(f32[32,128,1]{1,0,2:T(8,128)S(1)} %copy.33), channel_id=1, source_target_pairs={{1,0},{2,1},{3,2},{4,3},{5,4},{6,5},{7,6},{8,7},{9,8},{10,9},{11,1... | collective-permute-start | bytes 49160 | tf_op jit(solution)/shard_map/ppermute | solution.py:21
  113.0 8.4 %collective-permute-start.14 = (f32[32,1,130]{2,0,1:T(8,128)S(1)}, f32[32,1,130]{2,0,1:T(8,128)S(1)}, u32[]{:S(2)}, u32[]{:S(2)}) collective-permute-start(f32[32,1,130]{2,0,1:T(8,128)S(1)} %get-tuple-element.16), channel_id=1, source_target_pairs={{0,16},{16,32},{32,48},{48,64},{64,80},{80,96},{96,112},{1,17},{17... | collective-permute-start | bytes 49928 | tf_op jit(solution)/shard_map/ppermute | solution.py:19
  115.0 8.2 %collective-permute-start.15 = (f32[32,1,130]{2,0,1:T(8,128)S(1)}, f32[32,1,130]{2,0,1:T(8,128)S(1)}, u32[]{:S(2)}, u32[]{:S(2)}) collective-permute-start(f32[32,1,130]{2,0,1:T(8,128)S(1)} %get-tuple-element.17), channel_id=1, source_target_pairs={{16,0},{32,16},{48,32},{64,48},{80,64},{96,80},{112,96},{17,1},{33... | collective-permute-start | bytes 49928 | tf_op jit(solution)/shard_map/ppermute | solution.py:21
  144.3 9.9 %collective-permute-start.16 = (f32[32,128,1]{1,0,2:T(8,128)S(1)}, f32[32,128,1]{1,0,2:T(8,128)S(1)}, u32[]{:S(2)}, u32[]{:S(2)}) collective-permute-start(f32[32,128,1]{1,0,2:T(8,128)S(1)} %copy.37), channel_id=1, source_target_pairs={{0,1},{1,2},{2,3},{3,4},{4,5},{5,6},{6,7},{7,8},{8,9},{9,10},{10,1... | collective-permute-start | bytes 49160 | tf_op jit(solution)/shard_map/ppermute | solution.py:19
  147.0 10.1 %collective-permute-start.17 = (f32[32,128,1]{1,0,2:T(8,128)S(1)}, f32[32,128,1]{1,0,2:T(8,128)S(1)}, u32[]{:S(2)}, u32[]{:S(2)}) collective-permute-start(f32[32,128,1]{1,0,2:T(8,128)S(1)} %copy.38), channel_id=1, source_target_pairs={{1,0},{2,1},{3,2},{4,3},{5,4},{6,5},{7,6},{8,7},{9,8},{10,9},{11,1... | collective-permute-start | bytes 49160 | tf_op jit(solution)/shard_map/ppermute | solution.py:21
  161.0 8.1 %collective-permute-start.18 = (f32[32,1,130]{2,0,1:T(8,128)S(1)}, f32[32,1,130]{2,0,1:T(8,128)S(1)}, u32[]{:S(2)}, u32[]{:S(2)}) collective-permute-start(f32[32,1,130]{2,0,1:T(8,128)S(1)} %get-tuple-element.14), channel_id=1, source_target_pairs={{0,16},{16,32},{32,48},{48,64},{64,80},{80,96},{96,112},{1,17},{17... | collective-permute-start | bytes 49928 | tf_op jit(solution)/shard_map/ppermute | solution.py:19
  163.4 8.2 %collective-permute-start.19 = (f32[32,1,130]{2,0,1:T(8,128)S(1)}, f32[32,1,130]{2,0,1:T(8,128)S(1)}, u32[]{:S(2)}, u32[]{:S(2)}) collective-permute-start(f32[32,1,130]{2,0,1:T(8,128)S(1)} %get-tuple-element.15), channel_id=1, source_target_pairs={{16,0},{32,16},{48,32},{64,48},{80,64},{96,80},{112,96},{17,1},{33... | collective-permute-start | bytes 49928 | tf_op jit(solution)/shard_map/ppermute | solution.py:21
  197.1 8.1 %collective-permute-start.20 = (f32[32,128,1]{1,0,2:T(8,128)S(1)}, f32[32,128,1]{1,0,2:T(8,128)S(1)}, u32[]{:S(2)}, u32[]{:S(2)}) collective-permute-start(f32[32,128,1]{1,0,2:T(8,128)S(1)} %copy.47), channel_id=1, source_target_pairs={{0,1},{1,2},{2,3},{3,4},{4,5},{5,6},{6,7},{7,8},{8,9},{9,10},{10,1... | collective-permute-start | bytes 49160 | tf_op jit(solution)/shard_map/ppermute | solution.py:19
  199.8 8.3 %collective-permute-start.21 = (f32[32,128,1]{1,0,2:T(8,128)S(1)}, f32[32,128,1]{1,0,2:T(8,128)S(1)}, u32[]{:S(2)}, u32[]{:S(2)}) collective-permute-start(f32[32,128,1]{1,0,2:T(8,128)S(1)} %copy.48), channel_id=1, source_target_pairs={{1,0},{2,1},{3,2},{4,3},{5,4},{6,5},{7,6},{8,7},{9,8},{10,9},{11,1... | collective-permute-start | bytes 49160 | tf_op jit(solution)/shard_map/ppermute | solution.py:21
  214.5 7.9 %collective-permute-start.23 = (f32[32,1,130]{2,0,1:T(8,128)S(1)}, f32[32,1,130]{2,0,1:T(8,128)S(1)}, u32[]{:S(2)}, u32[]{:S(2)}) collective-permute-start(f32[32,1,130]{2,0,1:T(8,128)S(1)} %get-tuple-element.13), channel_id=1, source_target_pairs={{16,0},{32,16},{48,32},{64,48},{80,64},{96,80},{112,96},{17,1},{33... | collective-permute-start | bytes 49928 | tf_op jit(solution)/shard_map/ppermute | solution.py:21
  232.6 10.8 %collective-permute-start.24 = (f32[32,128,1]{1,0,2:T(8,128)S(1)}, f32[32,128,1]{1,0,2:T(8,128)S(1)}, u32[]{:S(2)}, u32[]{:S(2)}) collective-permute-start(f32[32,128,1]{1,0,2:T(8,128)S(1)} %copy.51), channel_id=1, source_target_pairs={{0,1},{1,2},{2,3},{3,4},{4,5},{5,6},{6,7},{7,8},{8,9},{9,10},{10,1... | collective-permute-start | bytes 49160 | tf_op jit(solution)/shard_map/ppermute | solution.py:19
  235.3 11.1 %collective-permute-start.25 = (f32[32,128,1]{1,0,2:T(8,128)S(1)}, f32[32,128,1]{1,0,2:T(8,128)S(1)}, u32[]{:S(2)}, u32[]{:S(2)}) collective-permute-start(f32[32,128,1]{1,0,2:T(8,128)S(1)} %copy.52), channel_id=1, source_target_pairs={{1,0},{2,1},{3,2},{4,3},{5,4},{6,5},{7,6},{8,7},{9,8},{10,9},{11,1... | collective-permute-start | bytes 49160 | tf_op jit(solution)/shard_map/ppermute | solution.py:21
  250.3 7.6 %collective-permute-start.26 = (f32[32,1,130]{2,0,1:T(8,128)S(1)}, f32[32,1,130]{2,0,1:T(8,128)S(1)}, u32[]{:S(2)}, u32[]{:S(2)}) collective-permute-start(f32[32,1,130]{2,0,1:T(8,128)S(1)} %get-tuple-element.10), channel_id=1, source_target_pairs={{0,16},{16,32},{32,48},{48,64},{64,80},{80,96},{96,112},{1,17},{17... | collective-permute-start | bytes 49928 | tf_op jit(solution)/shard_map/ppermute | solution.py:19
  252.5 7.9 %collective-permute-start.27 = (f32[32,1,130]{2,0,1:T(8,128)S(1)}, f32[32,1,130]{2,0,1:T(8,128)S(1)}, u32[]{:S(2)}, u32[]{:S(2)}) collective-permute-start(f32[32,1,130]{2,0,1:T(8,128)S(1)} %get-tuple-element.11), channel_id=1, source_target_pairs={{16,0},{32,16},{48,32},{64,48},{80,64},{96,80},{112,96},{17,1},{33... | collective-permute-start | bytes 49928 | tf_op jit(solution)/shard_map/ppermute | solution.py:21
  270.6 9.1 %collective-permute-start.28 = (f32[32,128,1]{1,0,2:T(8,128)S(1)}, f32[32,128,1]{1,0,2:T(8,128)S(1)}, u32[]{:S(2)}, u32[]{:S(2)}) collective-permute-start(f32[32,128,1]{1,0,2:T(8,128)S(1)} %copy.55), channel_id=1, source_target_pairs={{0,1},{1,2},{2,3},{3,4},{4,5},{5,6},{6,7},{7,8},{8,9},{9,10},{10,1... | collective-permute-start | bytes 49160 | tf_op jit(solution)/shard_map/ppermute | solution.py:19
  273.3 9.3 %collective-permute-start.29 = (f32[32,128,1]{1,0,2:T(8,128)S(1)}, f32[32,128,1]{1,0,2:T(8,128)S(1)}, u32[]{:S(2)}, u32[]{:S(2)}) collective-permute-start(f32[32,128,1]{1,0,2:T(8,128)S(1)} %copy.56), channel_id=1, source_target_pairs={{1,0},{2,1},{3,2},{4,3},{5,4},{6,5},{7,6},{8,7},{9,8},{10,9},{11,1... | collective-permute-start | bytes 49160 | tf_op jit(solution)/shard_map/ppermute | solution.py:21
  286.5 7.3 %collective-permute-start.30 = (f32[32,1,130]{2,0,1:T(8,128)S(1)}, f32[32,1,130]{2,0,1:T(8,128)S(1)}, u32[]{:S(2)}, u32[]{:S(2)}) collective-permute-start(f32[32,1,130]{2,0,1:T(8,128)S(1)} %get-tuple-element.8), channel_id=1, source_target_pairs={{0,16},{16,32},{32,48},{48,64},{64,80},{80,96},{96,112},{1,17},{17... | collective-permute-start | bytes 49928 | tf_op jit(solution)/shard_map/ppermute | solution.py:19
  288.7 7.9 %collective-permute-start.31 = (f32[32,1,130]{2,0,1:T(8,128)S(1)}, f32[32,1,130]{2,0,1:T(8,128)S(1)}, u32[]{:S(2)}, u32[]{:S(2)}) collective-permute-start(f32[32,1,130]{2,0,1:T(8,128)S(1)} %get-tuple-element.9), channel_id=1, source_target_pairs={{16,0},{32,16},{48,32},{64,48},{80,64},{96,80},{112,96},{17,1},{33... | collective-permute-start | bytes 49928 | tf_op jit(solution)/shard_map/ppermute | solution.py:21
  306.8 73.8 %collective-permute-start.32 = (f32[32,128,1]{1,0,2:T(8,128)S(1)}, f32[32,128,1]{1,0,2:T(8,128)}, u32[]{:S(2)}, u32[]{:S(2)}) collective-permute-start(f32[32,128,1]{1,0,2:T(8,128)S(1)} %copy.59), channel_id=1, source_target_pairs={{0,1},{1,2},{2,3},{3,4},{4,5},{5,6},{6,7},{7,8},{8,9},{9,10},{10,1... | collective-permute-start | bytes 49160 | tf_op jit(solution)/shard_map/ppermute | solution.py:19
  310.1 74.1 %collective-permute-start.33 = (f32[32,128,1]{1,0,2:T(8,128)}, f32[32,128,1]{1,0,2:T(8,128)}, u32[]{:S(2)}, u32[]{:S(2)}) collective-permute-start(f32[32,128,1]{1,0,2:T(8,128)} %copy.60), channel_id=1, source_target_pairs={{1,0},{2,1},{3,2},{4,3},{5,4},{6,5},{7,6},{8,7},{9,8},{10,9},{11,1... | collective-permute-start | bytes 49160 | tf_op jit(solution)/shard_map/ppermute | solution.py:21
  393.3 7.9 %collective-permute-start.35 = (f32[32,1,130]{2,0,1:T(8,128)S(1)}, f32[32,1,130]{2,0,1:T(8,128)S(1)}, u32[]{:S(2)}, u32[]{:S(2)}) collective-permute-start(f32[32,1,130]{2,0,1:T(8,128)S(1)} %get-tuple-element.7), channel_id=1, source_target_pairs={{16,0},{32,16},{48,32},{64,48},{80,64},{96,80},{112,96},{17,1},{33... | collective-permute-start | bytes 49928 | tf_op jit(solution)/shard_map/ppermute | solution.py:21
  (43 other events, 377.8 us)
where the time goes:
time: 415 us; the launch traced here: 408 us
  local copies, waits for them, and re-layouts  116 us (28%)
  starting transfers between devices  106 us (26%)
  other arithmetic  63.1 us (15%)
  blocking collectives  62.9 us (15%)
  matrix products  30.9 us (7%)
  waiting for transfers between devices  28 us (7%)
    ppermute x18, starting transfers between devices, padded_2(): lax.ppermute(head, axis, [((i + 1) % count, i) for i in range(ends)])  81.6 us
    psum x1, blocking collectives, local(): summed = lax.psum(weight_terms, ('lat', 'lon'))  62.9 us
    slice x17, local copies, waits for them, and re-layouts, padded_2(): lax.slice_in_dim(cells, cells.shape[dim] - width, cells.shape[dim], axis=...  44.4 us
    ppermute x18, waiting for transfers between devices, padded_2(): lax.ppermute(head, axis, [((i + 1) % count, i) for i in range(ends)])  28 us
    mul x9, other arithmetic, laplace(): return -scale_zero * neigh_sum(scale_one * padded, 1, 0)  24.9 us
    ppermute x18, starting transfers between devices, padded_2(): lax.ppermute(tail, axis, [(i, (i + 1) % count) for i in range(ends)])  24.2 us
    ppermute x8, local copies, waits for them, and re-layouts, padded_2(): lax.ppermute(tail, axis, [(i, (i + 1) % count) for i in range(ends)])  24 us
    ppermute x8, local copies, waits for them, and re-layouts, padded_2(): lax.ppermute(head, axis, [((i + 1) % count, i) for i in range(ends)])  23.6 us
  transfers between devices with their start and end apart: 36, of which 8 were waited for; matrix products, arithmetic and copies ran while one was open for 17% of the time, Pallas kernels for 0%

commit v1 on v0

--- a/solution.py
+++ b/solution.py
@@ -89,7 +89,8 @@
             for kept in carried
         ]
     )
-    summed = lax.psum(weight_terms, ("lat", "lon"))
+    parts = lax.all_gather(weight_terms, ("lat", "lon"), axis=0, tiled=False)
+    summed = parts.sum(axis=0)
     grid_cells = features.shape[1] * lax.axis_size("lat") * features.shape[2] * lax.axis_size("lon")
     weight_grad = summed * (1.0 / math.sqrt(grid_cells))
 

time: 415 us -> 431 us (1.039)
  the two profiles are of different devices: /device:TPU:96 before, /device:TPU:1 now
where the time goes in v1:
time: 431 us; the launch traced here: 424 us
  local copies, waits for them, and re-layouts  113 us (26%)
  starting transfers between devices  104 us (24%)
  waiting for transfers between devices  97 us (23%)
  other arithmetic  68 us (16%)
  matrix products  26.5 us (6%)
  between operations  15 us (3%)
    all_gather x1, waiting for transfers between devices, local(): parts = lax.all_gather(weight_terms, ('lat', 'lon'), axis=0, tiled=False)  71.4 us
    ppermute x18, starting transfers between devices, padded_2(): lax.ppermute(head, axis, [((i + 1) % count, i) for i in range(ends)])  61.9 us
    slice x17, local copies, waits for them, and re-layouts, padded_2(): lax.slice_in_dim(cells, cells.shape[dim] - width, cells.shape[dim], axis=...  43.6 us
    ppermute x18, starting transfers between devices, padded_2(): lax.ppermute(tail, axis, [(i, (i + 1) % count) for i in range(ends)])  42 us
    ppermute x18, waiting for transfers between devices, padded_2(): lax.ppermute(head, axis, [((i + 1) % count, i) for i in range(ends)])  25.5 us
    mul x9, other arithmetic, laplace(): return -scale_zero * neigh_sum(scale_one * padded, 1, 0)  24.8 us
    ppermute x8, local copies, waits for them, and re-layouts, padded_2(): lax.ppermute(tail, axis, [(i, (i + 1) % count) for i in range(ends)])  23.1 us
    ppermute x8, local copies, waits for them, and re-layouts, padded_2(): lax.ppermute(head, axis, [((i + 1) % count, i) for i in range(ends)])  22.9 us
  transfers between devices with their start and end apart: 37, of which 10 were waited for; matrix products, arithmetic and copies ran while one was open for 27% of the time, Pallas kernels for 0%

profile of v1, /device:TPU:1, one launch (start us, length us, event | category | flops | bytes accessed | tf_op | source)
XLA Modules:
  0.0 423.9 jit_solution(9618326960962907177)
XLA Ops:
  15.1 3.5 collective-permute-start.2
  38.5 4.4 %collective-permute-start.6 = (f32[32,1,130]{2,0,1:T(8,128)S(1)}, f32[32,1,130]{2,0,1:T(8,128)S(1)}, u32[]{:S(2)}, u32[]{:S(2)}) collective-permute-start(f32[32,1,130]{2,0,1:T(8,128)S(1)} %get-tuple-element.20), channel_id=1, source_target_pairs={{0,16},{16,32},{32,48},{48,64},{64,80},{80,96},{96,112},{1,17},{17... | collective-permute-start | bytes 49928 | tf_op jit(solution)/shard_map/ppermute | solution.py:19
  44.6 3.2 collective-permute-done.7
  61.2 6.1 %collective-permute-start.9 = (f32[32,128,1]{1,0,2:T(8,128)S(1)}, f32[32,128,1]{1,0,2:T(8,128)S(1)}, u32[]{:S(2)}, u32[]{:S(2)}) collective-permute-start(f32[32,128,1]{1,0,2:T(8,128)S(1)} %copy.28), channel_id=1, source_target_pairs={{1,0},{2,1},{3,2},{4,3},{5,4},{6,5},{7,6},{8,7},{9,8},{10,9},{11,1... | collective-permute-start | bytes 49160 | tf_op jit(solution)/shard_map/ppermute | solution.py:21
  67.3 2.9 copy.29
  74.1 3.7 collective-permute-start.10
  79.5 3.3 collective-permute-done.11
  85.2 4.1 fusion.25
  97.6 6.7 %collective-permute-start.13 = (f32[32,128,1]{1,0,2:T(8,128)S(1)}, f32[32,128,1]{1,0,2:T(8,128)S(1)}, u32[]{:S(2)}, u32[]{:S(2)}) collective-permute-start(f32[32,128,1]{1,0,2:T(8,128)S(1)} %copy.33), channel_id=1, source_target_pairs={{1,0},{2,1},{3,2},{4,3},{5,4},{6,5},{7,6},{8,7},{9,8},{10,9},{11,1... | collective-permute-start | bytes 49160 | tf_op jit(solution)/shard_map/ppermute | solution.py:21
  106.4 2.9 copy.34
  113.2 5.6 %collective-permute-start.14 = (f32[32,1,130]{2,0,1:T(8,128)S(1)}, f32[32,1,130]{2,0,1:T(8,128)S(1)}, u32[]{:S(2)}, u32[]{:S(2)}) collective-permute-start(f32[32,1,130]{2,0,1:T(8,128)S(1)} %get-tuple-element.16), channel_id=1, source_target_pairs={{0,16},{16,32},{32,48},{48,64},{64,80},{80,96},{96,112},{1,17},{17... | collective-permute-start | bytes 49928 | tf_op jit(solution)/shard_map/ppermute | solution.py:19
  124.0 3.8 maximum_multiply_fusion.2
  127.9 11.7 %fusion.22 = f32[32,128,128]{2,0,1:T(8,128)S(1)} fusion(f32[32,130,130]{2,0,1:T(8,128)} %maximum_multiply_fusion.2, f32[128,128]{1,0:T(8,128)S(1)} %slice_negate_fusion, f32[32,130,130]{2,0,1:T(8,128)S(1)} %bitcast.103), kind=kLoop, calls=%fused_computation.56 | loop fusion | flops 7340032 | bytes 27328512 | tf_op jit(solution)/shard_map/sub | solution.py:76
  147.7 6.5 %collective-permute-start.17 = (f32[32,128,1]{1,0,2:T(8,128)S(1)}, f32[32,128,1]{1,0,2:T(8,128)S(1)}, u32[]{:S(2)}, u32[]{:S(2)}) collective-permute-start(f32[32,128,1]{1,0,2:T(8,128)S(1)} %copy.38), channel_id=1, source_target_pairs={{1,0},{2,1},{3,2},{4,3},{5,4},{6,5},{7,6},{8,7},{9,8},{10,9},{11,1... | collective-permute-start | bytes 49160 | tf_op jit(solution)/shard_map/ppermute | solution.py:21
  162.9 3.7 collective-permute-start.18
  171.9 3.8 maximum_multiply_fusion.3
  175.7 10.2 %fusion.19 = bf16[32,128,128]{2,0,1:T(8,128)(2,1)S(1)} fusion(f32[32,128,128]{2,0,1:T(8,128)S(1)} %fusion.25, f32[32,130,130]{2,0,1:T(8,128)} %maximum_multiply_fusion.3, f32[128,128]{1,0:T(8,128)S(1)} %slice_negate_fusion), kind=kLoop, calls=%fused_computation.48 | loop fusion | flops 4718592 | bytes 15794176 | tf_op jit(solution)/shard_map/convert_element_type | solution.py:68
  185.9 5.3 %fusion.27 = bf16[32,128,128]{2,0,1:T(8,128)(2,1)S(1)} fusion(f32[128,128,32]{1,2,0:T(8,128)} %fusion.34, f32[128,128,32]{1,2,0:T(8,128)} %fusion.37, f32[128,128,32]{1,2,0:T(8,128)} %fusion.43, f32[128,128,32]{1,2,0:T(8,128)} %fusion.40, bf16[32,128,128]{2,0,1:T(8,128)(2,1)S(1)} %fusion.19, bf16[32,128,128]{2,1,0:T(8,128)(2,1)} %param.5, ...), kind=kOutput, calls=%fused_computation.76 | convolution fusion | flops 38273024 | bytes 11542528 | tf_op jit(solution)/shard_map/cd,cij->dij/dot_general | solution.py:81
  205.9 6.7 %collective-permute-start.21 = (f32[32,128,1]{1,0,2:T(8,128)S(1)}, f32[32,128,1]{1,0,2:T(8,128)S(1)}, u32[]{:S(2)}, u32[]{:S(2)}) collective-permute-start(f32[32,128,1]{1,0,2:T(8,128)S(1)} %copy.48), channel_id=1, source_target_pairs={{1,0},{2,1},{3,2},{4,3},{5,4},{6,5},{7,6},{8,7},{9,8},{10,9},{11,1... | collective-permute-start | bytes 49160 | tf_op jit(solution)/shard_map/ppermute | solution.py:21
  219.5 3.9 collective-permute-start.22
  224.7 3.6 collective-permute-done.23
  241.1 6.5 %collective-permute-start.25 = (f32[32,128,1]{1,0,2:T(8,128)S(1)}, f32[32,128,1]{1,0,2:T(8,128)S(1)}, u32[]{:S(2)}, u32[]{:S(2)}) collective-permute-start(f32[32,128,1]{1,0,2:T(8,128)S(1)} %copy.52), channel_id=1, source_target_pairs={{1,0},{2,1},{3,2},{4,3},{5,4},{6,5},{7,6},{8,7},{9,8},{10,9},{11,1... | collective-permute-start | bytes 49160 | tf_op jit(solution)/shard_map/ppermute | solution.py:21
  254.5 4.4 %collective-permute-start.26 = (f32[32,1,130]{2,0,1:T(8,128)S(1)}, f32[32,1,130]{2,0,1:T(8,128)S(1)}, u32[]{:S(2)}, u32[]{:S(2)}) collective-permute-start(f32[32,1,130]{2,0,1:T(8,128)S(1)} %get-tuple-element.10), channel_id=1, source_target_pairs={{0,16},{16,32},{32,48},{48,64},{64,80},{80,96},{96,112},{1,17},{17... | collective-permute-start | bytes 49928 | tf_op jit(solution)/shard_map/ppermute | solution.py:19
  260.5 4.3 %collective-permute-done.27 = f32[32,1,130]{2,0,1:T(8,128)S(1)} collective-permute-done((f32[32,1,130]{2,0,1:T(8,128)S(1)}, f32[32,1,130]{2,0,1:T(8,128)S(1)}, u32[]{:S(2)}, u32[]{:S(2)}) %collective-permute-start.27) | collective-permute-done | bytes 16672 | tf_op jit(solution)/shard_map/ppermute | solution.py:21
  275.7 6.1 %collective-permute-start.29 = (f32[32,128,1]{1,0,2:T(8,128)S(1)}, f32[32,128,1]{1,0,2:T(8,128)S(1)}, u32[]{:S(2)}, u32[]{:S(2)}) collective-permute-start(f32[32,128,1]{1,0,2:T(8,128)S(1)} %copy.56), channel_id=1, source_target_pairs={{1,0},{2,1},{3,2},{4,3},{5,4},{6,5},{7,6},{8,7},{9,8},{10,9},{11,1... | collective-permute-start | bytes 49160 | tf_op jit(solution)/shard_map/ppermute | solution.py:21
  288.5 4.6 %collective-permute-start.30 = (f32[32,1,130]{2,0,1:T(8,128)S(1)}, f32[32,1,130]{2,0,1:T(8,128)S(1)}, u32[]{:S(2)}, u32[]{:S(2)}) collective-permute-start(f32[32,1,130]{2,0,1:T(8,128)S(1)} %get-tuple-element.8), channel_id=1, source_target_pairs={{0,16},{16,32},{32,48},{48,64},{64,80},{80,96},{96,112},{1,17},{17... | collective-permute-start | bytes 49928 | tf_op jit(solution)/shard_map/ppermute | solution.py:19
  294.7 3.6 collective-permute-done.31
  311.2 6.6 %collective-permute-start.33 = (f32[32,128,1]{1,0,2:T(8,128)S(1)}, f32[32,128,1]{1,0,2:T(8,128)S(1)}, u32[]{:S(2)}, u32[]{:S(2)}) collective-permute-start(f32[32,128,1]{1,0,2:T(8,128)S(1)} %copy.60), channel_id=1, source_target_pairs={{1,0},{2,1},{3,2},{4,3},{5,4},{6,5},{7,6},{8,7},{9,8},{10,9},{11,1... | collective-permute-start | bytes 49160 | tf_op jit(solution)/shard_map/ppermute | solution.py:21
  324.6 3.8 collective-permute-start.34
  330.0 3.3 collective-permute-done.35
  339.5 71.4 %all-gather.3.cloned.1.call-done = f32[640,32,32]{2,1,0:T(8,128)} async-done(((f32[5,32,32]{2,1,0:T(8,128)}), f32[640,32,32]{2,1,0:T(8,128)}) %all-gather.3.cloned.1.call-update) | async-done | bytes 2621456 | tf_op jit(solution)/shard_map/all_gather | solution.py:92
  411.0 5.2 %reduce_sum.9 = f32[5,32,32]{2,1,0:T(8,128)S(1)} reduce(f32[128,5,32,32]{3,2,1,0:T(8,128)} %bitcast.104, f32[]{:T(128)} %constant.1.clone.1), dimensions={0}, to_apply=%region_0.0 | reduce | flops 650240 | bytes 2641924 | tf_op jit(solution)/shard_map/reduce_sum | solution.py:93
  (208 shorter events, 183.5 us)
Async XLA Ops:
  7.2 403.8 %all-gather.3.cloned.1.call-start = ((), (), s32[]{:S(2)}) async-start(), calls=%async_computation | async-start | bytes 10567680 | tf_op jit(solution)/shard_map/all_gather | solution.py:92
  8.2 5.6 %collective-permute-start = (s32[128,3]{1,0:T(8,128)S(1)}, s32[128,3]{1,0:T(8,128)S(1)}, u32[]{:S(2)}, u32[]{:S(2)}) collective-permute-start(s32[128,3]{1,0:T(8,128)S(1)} %get-tuple-element.40), channel_id=1, source_target_pairs={{0,1},{1,2},{2,3},{3,4},{4,5},{5,6},{6,7},{7,8},{8,9},{9,10},{10,1... | collective-permute-start | bytes 4616 | tf_op jit(solution)/shard_map/ppermute | solution.py:19
  15.1 16.3 %collective-permute-start.2 = (s32[3,134]{1,0:T(4,128)S(1)}, s32[3,134]{1,0:T(4,128)S(1)}, u32[]{:S(2)}, u32[]{:S(2)}) collective-permute-start(s32[3,134]{1,0:T(4,128)S(1)} %get-tuple-element.38), channel_id=1, source_target_pairs={{0,16},{16,32},{32,48},{48,64},{64,80},{80,96},{96,112},{1,17},{17... | collective-permute-start | bytes 4832 | tf_op jit(solution)/shard_map/ppermute | solution.py:19
  18.6 12.8 %collective-permute-start.3 = (s32[3,134]{1,0:T(4,128)S(1)}, s32[3,134]{1,0:T(4,128)S(1)}, u32[]{:S(2)}, u32[]{:S(2)}) collective-permute-start(s32[3,134]{1,0:T(4,128)S(1)} %get-tuple-element.39), channel_id=1, source_target_pairs={{16,0},{32,16},{48,32},{64,48},{80,64},{96,80},{112,96},{17,1},{33... | collective-permute-start | bytes 4832 | tf_op jit(solution)/shard_map/ppermute | solution.py:21
  25.3 6.5 %collective-permute-start.4 = (f32[32,128,1]{1,0,2:T(8,128)S(1)}, f32[32,128,1]{1,0,2:T(8,128)S(1)}, u32[]{:S(2)}, u32[]{:S(2)}) collective-permute-start(f32[32,128,1]{1,0,2:T(8,128)S(1)} %copy.22), channel_id=1, source_target_pairs={{0,1},{1,2},{2,3},{3,4},{4,5},{5,6},{6,7},{7,8},{8,9},{9,10},{10,1... | collective-permute-start | bytes 49160 | tf_op jit(solution)/shard_map/ppermute | solution.py:19
  28.9 5.8 %collective-permute-start.5 = (f32[32,128,1]{1,0,2:T(8,128)S(1)}, f32[32,128,1]{1,0,2:T(8,128)S(1)}, u32[]{:S(2)}, u32[]{:S(2)}) collective-permute-start(f32[32,128,1]{1,0,2:T(8,128)S(1)} %copy.23), channel_id=1, source_target_pairs={{1,0},{2,1},{3,2},{4,3},{5,4},{6,5},{7,6},{8,7},{9,8},{10,9},{11,1... | collective-permute-start | bytes 49160 | tf_op jit(solution)/shard_map/ppermute | solution.py:21
  38.5 6.1 %collective-permute-start.6 = (f32[32,1,130]{2,0,1:T(8,128)S(1)}, f32[32,1,130]{2,0,1:T(8,128)S(1)}, u32[]{:S(2)}, u32[]{:S(2)}) collective-permute-start(f32[32,1,130]{2,0,1:T(8,128)S(1)} %get-tuple-element.20), channel_id=1, source_target_pairs={{0,16},{16,32},{32,48},{48,64},{64,80},{80,96},{96,112},{1,17},{17... | collective-permute-start | bytes 49928 | tf_op jit(solution)/shard_map/ppermute | solution.py:19
  57.9 9.3 %collective-permute-start.8 = (f32[32,128,1]{1,0,2:T(8,128)S(1)}, f32[32,128,1]{1,0,2:T(8,128)S(1)}, u32[]{:S(2)}, u32[]{:S(2)}) collective-permute-start(f32[32,128,1]{1,0,2:T(8,128)S(1)} %copy.27), channel_id=1, source_target_pairs={{0,1},{1,2},{2,3},{3,4},{4,5},{5,6},{6,7},{7,8},{8,9},{9,10},{10,1... | collective-permute-start | bytes 49160 | tf_op jit(solution)/shard_map/ppermute | solution.py:19
  61.2 9.0 %collective-permute-start.9 = (f32[32,128,1]{1,0,2:T(8,128)S(1)}, f32[32,128,1]{1,0,2:T(8,128)S(1)}, u32[]{:S(2)}, u32[]{:S(2)}) collective-permute-start(f32[32,128,1]{1,0,2:T(8,128)S(1)} %copy.28), channel_id=1, source_target_pairs={{1,0},{2,1},{3,2},{4,3},{5,4},{6,5},{7,6},{8,7},{9,8},{10,9},{11,1... | collective-permute-start | bytes 49160 | tf_op jit(solution)/shard_map/ppermute | solution.py:21
  74.1 5.3 %collective-permute-start.10 = (f32[32,1,130]{2,0,1:T(8,128)S(1)}, f32[32,1,130]{2,0,1:T(8,128)S(1)}, u32[]{:S(2)}, u32[]{:S(2)}) collective-permute-start(f32[32,1,130]{2,0,1:T(8,128)S(1)} %get-tuple-element.18), channel_id=1, source_target_pairs={{0,16},{16,32},{32,48},{48,64},{64,80},{80,96},{96,112},{1,17},{17... | collective-permute-start | bytes 49928 | tf_op jit(solution)/shard_map/ppermute | solution.py:19
  94.8 11.5 %collective-permute-start.12 = (f32[32,128,1]{1,0,2:T(8,128)S(1)}, f32[32,128,1]{1,0,2:T(8,128)S(1)}, u32[]{:S(2)}, u32[]{:S(2)}) collective-permute-start(f32[32,128,1]{1,0,2:T(8,128)S(1)} %copy.32), channel_id=1, source_target_pairs={{0,1},{1,2},{2,3},{3,4},{4,5},{5,6},{6,7},{7,8},{8,9},{9,10},{10,1... | collective-permute-start | bytes 49160 | tf_op jit(solution)/shard_map/ppermute | solution.py:19
  97.6 11.8 %collective-permute-start.13 = (f32[32,128,1]{1,0,2:T(8,128)S(1)}, f32[32,128,1]{1,0,2:T(8,128)S(1)}, u32[]{:S(2)}, u32[]{:S(2)}) collective-permute-start(f32[32,128,1]{1,0,2:T(8,128)S(1)} %copy.33), channel_id=1, source_target_pairs={{1,0},{2,1},{3,2},{4,3},{5,4},{6,5},{7,6},{8,7},{9,8},{10,9},{11,1... | collective-permute-start | bytes 49160 | tf_op jit(solution)/shard_map/ppermute | solution.py:21
  113.2 9.4 %collective-permute-start.14 = (f32[32,1,130]{2,0,1:T(8,128)S(1)}, f32[32,1,130]{2,0,1:T(8,128)S(1)}, u32[]{:S(2)}, u32[]{:S(2)}) collective-permute-start(f32[32,1,130]{2,0,1:T(8,128)S(1)} %get-tuple-element.16), channel_id=1, source_target_pairs={{0,16},{16,32},{32,48},{48,64},{64,80},{80,96},{96,112},{1,17},{17... | collective-permute-start | bytes 49928 | tf_op jit(solution)/shard_map/ppermute | solution.py:19
  118.8 5.2 %collective-permute-start.15 = (f32[32,1,130]{2,0,1:T(8,128)S(1)}, f32[32,1,130]{2,0,1:T(8,128)S(1)}, u32[]{:S(2)}, u32[]{:S(2)}) collective-permute-start(f32[32,1,130]{2,0,1:T(8,128)S(1)} %get-tuple-element.17), channel_id=1, source_target_pairs={{16,0},{32,16},{48,32},{64,48},{80,64},{96,80},{112,96},{17,1},{33... | collective-permute-start | bytes 49928 | tf_op jit(solution)/shard_map/ppermute | solution.py:21
  145.0 11.2 %collective-permute-start.16 = (f32[32,128,1]{1,0,2:T(8,128)S(1)}, f32[32,128,1]{1,0,2:T(8,128)S(1)}, u32[]{:S(2)}, u32[]{:S(2)}) collective-permute-start(f32[32,128,1]{1,0,2:T(8,128)S(1)} %copy.37), channel_id=1, source_target_pairs={{0,1},{1,2},{2,3},{3,4},{4,5},{5,6},{6,7},{7,8},{8,9},{9,10},{10,1... | collective-permute-start | bytes 49160 | tf_op jit(solution)/shard_map/ppermute | solution.py:19
  147.7 11.3 %collective-permute-start.17 = (f32[32,128,1]{1,0,2:T(8,128)S(1)}, f32[32,128,1]{1,0,2:T(8,128)S(1)}, u32[]{:S(2)}, u32[]{:S(2)}) collective-permute-start(f32[32,128,1]{1,0,2:T(8,128)S(1)} %copy.38), channel_id=1, source_target_pairs={{1,0},{2,1},{3,2},{4,3},{5,4},{6,5},{7,6},{8,7},{9,8},{10,9},{11,1... | collective-permute-start | bytes 49160 | tf_op jit(solution)/shard_map/ppermute | solution.py:21
  162.9 7.3 %collective-permute-start.18 = (f32[32,1,130]{2,0,1:T(8,128)S(1)}, f32[32,1,130]{2,0,1:T(8,128)S(1)}, u32[]{:S(2)}, u32[]{:S(2)}) collective-permute-start(f32[32,1,130]{2,0,1:T(8,128)S(1)} %get-tuple-element.14), channel_id=1, source_target_pairs={{0,16},{16,32},{32,48},{48,64},{64,80},{80,96},{96,112},{1,17},{17... | collective-permute-start | bytes 49928 | tf_op jit(solution)/shard_map/ppermute | solution.py:19
  166.7 5.2 %collective-permute-start.19 = (f32[32,1,130]{2,0,1:T(8,128)S(1)}, f32[32,1,130]{2,0,1:T(8,128)S(1)}, u32[]{:S(2)}, u32[]{:S(2)}) collective-permute-start(f32[32,1,130]{2,0,1:T(8,128)S(1)} %get-tuple-element.15), channel_id=1, source_target_pairs={{16,0},{32,16},{48,32},{64,48},{80,64},{96,80},{112,96},{17,1},{33... | collective-permute-start | bytes 49928 | tf_op jit(solution)/shard_map/ppermute | solution.py:21
  203.2 9.4 %collective-permute-start.20 = (f32[32,128,1]{1,0,2:T(8,128)S(1)}, f32[32,128,1]{1,0,2:T(8,128)S(1)}, u32[]{:S(2)}, u32[]{:S(2)}) collective-permute-start(f32[32,128,1]{1,0,2:T(8,128)S(1)} %copy.47), channel_id=1, source_target_pairs={{0,1},{1,2},{2,3},{3,4},{4,5},{5,6},{6,7},{7,8},{8,9},{9,10},{10,1... | collective-permute-start | bytes 49160 | tf_op jit(solution)/shard_map/ppermute | solution.py:19
  205.9 9.6 %collective-permute-start.21 = (f32[32,128,1]{1,0,2:T(8,128)S(1)}, f32[32,128,1]{1,0,2:T(8,128)S(1)}, u32[]{:S(2)}, u32[]{:S(2)}) collective-permute-start(f32[32,128,1]{1,0,2:T(8,128)S(1)} %copy.48), channel_id=1, source_target_pairs={{1,0},{2,1},{3,2},{4,3},{5,4},{6,5},{7,6},{8,7},{9,8},{10,9},{11,1... | collective-permute-start | bytes 49160 | tf_op jit(solution)/shard_map/ppermute | solution.py:21
  219.5 5.2 %collective-permute-start.22 = (f32[32,1,130]{2,0,1:T(8,128)S(1)}, f32[32,1,130]{2,0,1:T(8,128)S(1)}, u32[]{:S(2)}, u32[]{:S(2)}) collective-permute-start(f32[32,1,130]{2,0,1:T(8,128)S(1)} %get-tuple-element.12), channel_id=1, source_target_pairs={{0,16},{16,32},{32,48},{48,64},{64,80},{80,96},{96,112},{1,17},{17... | collective-permute-start | bytes 49928 | tf_op jit(solution)/shard_map/ppermute | solution.py:19
  238.4 9.3 %collective-permute-start.24 = (f32[32,128,1]{1,0,2:T(8,128)S(1)}, f32[32,128,1]{1,0,2:T(8,128)S(1)}, u32[]{:S(2)}, u32[]{:S(2)}) collective-permute-start(f32[32,128,1]{1,0,2:T(8,128)S(1)} %copy.51), channel_id=1, source_target_pairs={{0,1},{1,2},{2,3},{3,4},{4,5},{5,6},{6,7},{7,8},{8,9},{9,10},{10,1... | collective-permute-start | bytes 49160 | tf_op jit(solution)/shard_map/ppermute | solution.py:19
  241.1 9.4 %collective-permute-start.25 = (f32[32,128,1]{1,0,2:T(8,128)S(1)}, f32[32,128,1]{1,0,2:T(8,128)S(1)}, u32[]{:S(2)}, u32[]{:S(2)}) collective-permute-start(f32[32,128,1]{1,0,2:T(8,128)S(1)} %copy.52), channel_id=1, source_target_pairs={{1,0},{2,1},{3,2},{4,3},{5,4},{6,5},{7,6},{8,7},{9,8},{10,9},{11,1... | collective-permute-start | bytes 49160 | tf_op jit(solution)/shard_map/ppermute | solution.py:21
  254.5 6.1 %collective-permute-start.26 = (f32[32,1,130]{2,0,1:T(8,128)S(1)}, f32[32,1,130]{2,0,1:T(8,128)S(1)}, u32[]{:S(2)}, u32[]{:S(2)}) collective-permute-start(f32[32,1,130]{2,0,1:T(8,128)S(1)} %get-tuple-element.10), channel_id=1, source_target_pairs={{0,16},{16,32},{32,48},{48,64},{64,80},{80,96},{96,112},{1,17},{17... | collective-permute-start | bytes 49928 | tf_op jit(solution)/shard_map/ppermute | solution.py:19
  258.8 6.0 %collective-permute-start.27 = (f32[32,1,130]{2,0,1:T(8,128)S(1)}, f32[32,1,130]{2,0,1:T(8,128)S(1)}, u32[]{:S(2)}, u32[]{:S(2)}) collective-permute-start(f32[32,1,130]{2,0,1:T(8,128)S(1)} %get-tuple-element.11), channel_id=1, source_target_pairs={{16,0},{32,16},{48,32},{64,48},{80,64},{96,80},{112,96},{17,1},{33... | collective-permute-start | bytes 49928 | tf_op jit(solution)/shard_map/ppermute | solution.py:21
  274.3 7.4 %collective-permute-start.28 = (f32[32,128,1]{1,0,2:T(8,128)S(1)}, f32[32,128,1]{1,0,2:T(8,128)S(1)}, u32[]{:S(2)}, u32[]{:S(2)}) collective-permute-start(f32[32,128,1]{1,0,2:T(8,128)S(1)} %copy.55), channel_id=1, source_target_pairs={{0,1},{1,2},{2,3},{3,4},{4,5},{5,6},{6,7},{7,8},{8,9},{9,10},{10,1... | collective-permute-start | bytes 49160 | tf_op jit(solution)/shard_map/ppermute | solution.py:19
  275.7 8.9 %collective-permute-start.29 = (f32[32,128,1]{1,0,2:T(8,128)S(1)}, f32[32,128,1]{1,0,2:T(8,128)S(1)}, u32[]{:S(2)}, u32[]{:S(2)}) collective-permute-start(f32[32,128,1]{1,0,2:T(8,128)S(1)} %copy.56), channel_id=1, source_target_pairs={{1,0},{2,1},{3,2},{4,3},{5,4},{6,5},{7,6},{8,7},{9,8},{10,9},{11,1... | collective-permute-start | bytes 49160 | tf_op jit(solution)/shard_map/ppermute | solution.py:21
  288.5 6.2 %collective-permute-start.30 = (f32[32,1,130]{2,0,1:T(8,128)S(1)}, f32[32,1,130]{2,0,1:T(8,128)S(1)}, u32[]{:S(2)}, u32[]{:S(2)}) collective-permute-start(f32[32,1,130]{2,0,1:T(8,128)S(1)} %get-tuple-element.8), channel_id=1, source_target_pairs={{0,16},{16,32},{32,48},{48,64},{64,80},{80,96},{96,112},{1,17},{17... | collective-permute-start | bytes 49928 | tf_op jit(solution)/shard_map/ppermute | solution.py:19
  293.1 5.2 %collective-permute-start.31 = (f32[32,1,130]{2,0,1:T(8,128)S(1)}, f32[32,1,130]{2,0,1:T(8,128)S(1)}, u32[]{:S(2)}, u32[]{:S(2)}) collective-permute-start(f32[32,1,130]{2,0,1:T(8,128)S(1)} %get-tuple-element.9), channel_id=1, source_target_pairs={{16,0},{32,16},{48,32},{64,48},{80,64},{96,80},{112,96},{17,1},{33... | collective-permute-start | bytes 49928 | tf_op jit(solution)/shard_map/ppermute | solution.py:21
  308.5 9.3 %collective-permute-start.32 = (f32[32,128,1]{1,0,2:T(8,128)S(1)}, f32[32,128,1]{1,0,2:T(8,128)S(1)}, u32[]{:S(2)}, u32[]{:S(2)}) collective-permute-start(f32[32,128,1]{1,0,2:T(8,128)S(1)} %copy.59), channel_id=1, source_target_pairs={{0,1},{1,2},{2,3},{3,4},{4,5},{5,6},{6,7},{7,8},{8,9},{9,10},{10,1... | collective-permute-start | bytes 49160 | tf_op jit(solution)/shard_map/ppermute | solution.py:19
  311.2 9.5 %collective-permute-start.33 = (f32[32,128,1]{1,0,2:T(8,128)S(1)}, f32[32,128,1]{1,0,2:T(8,128)S(1)}, u32[]{:S(2)}, u32[]{:S(2)}) collective-permute-start(f32[32,128,1]{1,0,2:T(8,128)S(1)} %copy.60), channel_id=1, source_target_pairs={{1,0},{2,1},{3,2},{4,3},{5,4},{6,5},{7,6},{8,7},{9,8},{10,9},{11,1... | collective-permute-start | bytes 49160 | tf_op jit(solution)/shard_map/ppermute | solution.py:21
  324.6 5.4 %collective-permute-start.34 = (f32[32,1,130]{2,0,1:T(8,128)S(1)}, f32[32,1,130]{2,0,1:T(8,128)S(1)}, u32[]{:S(2)}, u32[]{:S(2)}) collective-permute-start(f32[32,1,130]{2,0,1:T(8,128)S(1)} %get-tuple-element.6), channel_id=1, source_target_pairs={{0,16},{16,32},{32,48},{48,64},{64,80},{80,96},{96,112},{1,17},{17... | collective-permute-start | bytes 49928 | tf_op jit(solution)/shard_map/ppermute | solution.py:19
  (44 other events, 329.4 us)
Sparse Core Ops, SparseCore 0:
  197.9 213.0 all-gather.2
